TPU v7x, 256 devices: a whole 4x4x8 slice. The times are simulated.
256 devices in a mesh: dp: 16 (over z, core), ctx: 4 (over x), head: 4 (over y).
Axes of the slice: x: 4, y: 4, z: 8, core: 2. Of those that a mesh axis runs over, the one named last changes fastest.
Arguments:
- hidden_in: bfloat16 [16, 2048, 8192], P('dp', 'ctx', 'head'), may hold values from -40 to 40
- w_query: bfloat16 [8192, 4096], P('dp', 'head'), may hold values from -0.0625 to 0.0625
- w_key: bfloat16 [8192, 512], P('dp', 'head'), may hold values from -0.0625 to 0.0625
- w_value: bfloat16 [8192, 512], P('dp', 'head'), may hold values from -0.0625 to 0.0625
- mem_gate: float32 [32], P('head'), may hold values from -3 to 3
Outputs:
- attended: bfloat16 [16, 2048, 4096], P('dp', 'ctx', 'head')
All inputs are finite; a program needn't handle non-finite values.
Results may differ from a plain program's by a relative error of at most 0.011.
Values may be sent and summed in bfloat16 or wider, within the bound.
A program may use at most 128 MiB of HBM per device.

v0:
```python
import math
import jax
import jax.numpy as jnp
from jax import lax
from jax.sharding import PartitionSpec as P

HD = 128
SEG = 128


def entering(shard, axis, combine, identity):
    peers, index = (lax.axis_size(axis), lax.axis_index(axis))
    everything = jax.tree.map(
        lambda part, kind: lax.all_gather(part.astype(kind), axis),
        shard,
        (jnp.bfloat16, jnp.bfloat16),
    )
    start = jax.tree.map(
        lambda part, zero: jnp.broadcast_to(jnp.asarray(zero, part.dtype), part.shape),
        shard,
        identity,
    )

    def lap(k, before):
        reached = k < index
        new = combine(
            before, jax.tree.map(lambda part, own: part[k].astype(own.dtype), everything, shard)
        )
        return jax.tree.map(lambda a, b: jnp.where(reached, a, b), new, before)

    return lax.fori_loop(0, peers, lap, start)


def feature_map(vector):
    return jax.nn.elu(vector) + 1.0


def exclusive_sum(stack):
    running = jnp.cumsum(stack, axis=0)
    return jnp.concatenate([jnp.zeros_like(stack[:1]), running[:-1]], axis=0)


def add_pair(earlier, later):
    return (earlier[0] + later[0], earlier[1] + later[1])


def body(hidden_in, w_query, w_key, w_value, mem_gate):
    highest = lax.Precision.HIGHEST
    features = lax.all_gather(hidden_in, "head", axis=2, tiled=True)
    tok_rows = features.shape[1]
    flattened = features[0]
    query_full = jnp.dot(
        flattened,
        lax.all_gather(w_query, "dp", axis=0, tiled=True),
        preferred_element_type=jnp.float32,
    )
    keys_full = jnp.dot(
        flattened,
        lax.all_gather(w_key, "dp", axis=0, tiled=True),
        preferred_element_type=jnp.float32,
    )
    values_full = jnp.dot(
        flattened,
        lax.all_gather(w_value, "dp", axis=0, tiled=True),
        preferred_element_type=jnp.float32,
    )
    query = query_full.astype(jnp.bfloat16)
    keys = keys_full.astype(jnp.bfloat16)
    values = values_full.astype(jnp.bfloat16)
    heads_dev = query.shape[1] // HD
    kv_dev = keys.shape[1] // HD
    group_size = heads_dev // kv_dev
    segments = tok_rows // SEG
    query_seg = query.reshape(segments, SEG, kv_dev, group_size, HD)
    key_seg = keys.reshape(segments, SEG, kv_dev, HD)
    value_seg = values.reshape(segments, SEG, kv_dev, HD)
    scores = jnp.einsum(
        "nqkgd,nskd->nkgqs", query_seg, key_seg, preferred_element_type=jnp.float32
    ) / math.sqrt(HD)
    causal = jnp.arange(SEG)[:, None] >= jnp.arange(SEG)[None, :]
    scores = jnp.where(causal, scores, -jnp.inf)
    probs = jax.nn.softmax(scores, axis=-1).astype(jnp.bfloat16)
    local = jnp.einsum("nkgqs,nskd->nqkgd", probs, value_seg, preferred_element_type=jnp.float32)
    value_wide = value_seg.astype(jnp.float32)
    feat_key = feature_map(key_seg.astype(jnp.float32))
    increment = jnp.einsum("nskd,nske->nkde", feat_key, value_wide, precision=highest)
    key_mass = jnp.sum(feat_key, axis=1)
    state_total = jnp.sum(increment, axis=0)
    mass_total = jnp.sum(key_mass, axis=0)
    prior_state, prior_mass = entering(
        (state_total, mass_total),
        "ctx",
        add_pair,
        (jnp.zeros_like(state_total), jnp.zeros_like(mass_total)),
    )
    memory = prior_state[None] + exclusive_sum(increment)
    mass_prior = prior_mass[None] + exclusive_sum(key_mass)
    feat_query = feature_map(query_seg.astype(jnp.float32))
    numerator = jnp.einsum("nqkgd,nkde->nqkge", feat_query, memory, precision=highest)
    denominator = jnp.einsum("nqkgd,nkd->nqkg", feat_query, mass_prior, precision=highest) + 1.0
    retrieved = numerator / denominator[..., None]
    gate_share = jax.nn.sigmoid(mem_gate).reshape(kv_dev, group_size)[None, None, :, :, None]
    mixed = gate_share * retrieved + (1.0 - gate_share) * local
    return mixed.reshape(1, tok_rows, heads_dev * HD).astype(jnp.bfloat16)


def solution(mesh):
    return jax.shard_map(
        body,
        mesh=mesh,
        in_specs=(
            P("dp", "ctx", "head"),
            P("dp", "head"),
            P("dp", "head"),
            P("dp", "head"),
            P("head"),
        ),
        out_specs=P("dp", "ctx", "head"),
        check_vma=False,
    )
```

profile of v0, /device:TPU:1, one launch (start us, length us, event | category | flops | bytes accessed | tf_op | source)
XLA Modules:
  0.0 307.1 jit_solution(8610718658696810357)
XLA Ops:
  6.5 0.0 all-gather.12.cloned.1.call-start
  6.5 0.7 all-gather.12.cloned.1.call-update
  7.3 0.0 all-gather.8.cloned.1.call-start
  7.3 0.7 all-gather.8.cloned.1.call-update
  8.0 0.0 all-gather.10.cloned.1.call-start
  8.1 0.7 all-gather.10.cloned.1.call-update
  8.7 0.0 all-gather.14.cloned.1.call-start
  8.8 0.5 all-gather.14.cloned.1.call-update
  9.4 43.4 %all-gather.12.cloned.1.call-done = bf16[8192,128]{1,0:T(8,128)(2,1)} async-done(((bf16[512,128]{1,0:T(8,128)(2,1)}), bf16[8192,128]{1,0:T(8,128)(2,1)}) %all-gather.12.cloned.1.call-update) | async-done | bytes 2097168 | tf_op jit(solution)/shard_map/all_gather | solution.py:64
  52.8 85.3 %all-gather.8.cloned.1.call-done = bf16[1,512,8192]{2,1,0:T(8,128)(2,1)} async-done(((bf16[1,512,2048]{2,1,0:T(8,128)(2,1)}), bf16[1,512,8192]{2,1,0:T(8,128)(2,1)}) %all-gather.8.cloned.1.call-update) | async-done | bytes 8388624 | tf_op jit(solution)/shard_map/all_gather | solution.py:49
  138.1 6.3 %fusion.24 = bf16[512,128]{1,0:T(8,128)(2,1)S(1)} fusion(bf16[8192,128]{1,0:T(8,128)(2,1)} %all-gather.12.cloned.1.call-done, bf16[1,512,8192]{2,1,0:T(8,128)(2,1)} %all-gather.8.cloned.1.call-done), kind=kOutput, calls=%fused_computation.27 | convolution fusion | flops 1073807360 | bytes 10616832 | tf_op jit(solution)/shard_map/dot_general | solution.py:62
  144.4 36.5 %all-gather.10.cloned.1.call-done = bf16[8192,128]{1,0:T(8,128)(2,1)} async-done(((bf16[512,128]{1,0:T(8,128)(2,1)}), bf16[8192,128]{1,0:T(8,128)(2,1)}) %all-gather.10.cloned.1.call-update) | async-done | bytes 2097168 | tf_op jit(solution)/shard_map/all_gather | solution.py:59
  180.9 6.3 %fusion.42 = (bf16[128]{0:T(256)(128)(2,1)S(1)}, bf16[512,128]{1,0:T(8,128)(2,1)S(1)}) fusion(bf16[8192,128]{1,0:T(8,128)(2,1)} %all-gather.10.cloned.1.call-done, bf16[1,512,8192]{2,1,0:T(8,128)(2,1)} %all-gather.8.cloned.1.call-done), kind=kOutput, calls=%fused_computation.48 | convolution fusion | flops 1074200448 | bytes 10617088 | tf_op jit(solution)/shard_map/dot_general | solution.py:57
  187.3 0.5 fusion.64
  187.7 0.2 fusion.47
  187.9 0.0 copy-start
  187.9 0.1 fusion.45
  188.1 7.6 %all-gather.2 = bf16[4,1,128]{2,1,0:T(2,128)(2,1)S(1)} all-gather(bf16[1,1,128]{2,1,0:T(2,128)(2,1)S(1)} %bitcast.115), channel_id=3, replica_groups=mesh['dp'=16,'ctx'=4,'head'=4] {'ctx'}, dimensions={0}, use_global_device_ids=true | all-gather | bytes 1280 | tf_op jit(solution)/shard_map/all_gather | solution.py:14
  195.7 10.5 %all-gather = bf16[512,128]{1,0:T(8,128)(2,1)S(1)} all-gather(bf16[128,128]{1,0:T(8,128)(2,1)S(1)} %get-tuple-element.152), channel_id=2, replica_groups=mesh['dp'=16,'ctx'=4,'head'=4] {'ctx'}, dimensions={0}, use_global_device_ids=true | all-gather | bytes 163840 | tf_op jit(solution)/shard_map/all_gather | solution.py:14
  206.2 0.2 while.16
  206.4 70.0 %all-gather.14.cloned.1.call-done = bf16[8192,1024]{1,0:T(8,128)(2,1)} async-done(((bf16[512,1024]{1,0:T(8,128)(2,1)}), bf16[8192,1024]{1,0:T(8,128)(2,1)}) %all-gather.14.cloned.1.call-update) | async-done | bytes 16777232 | tf_op jit(solution)/shard_map/all_gather | solution.py:54
  276.4 14.8 %fusion.18 = bf16[64,8,8,128]{3,1,2,0:T(8,128)(2,1)S(1)} fusion(bf16[8192,1024]{1,0:T(8,128)(2,1)} %all-gather.14.cloned.1.call-done, bf16[1,512,8192]{2,1,0:T(8,128)(2,1)} %all-gather.8.cloned.1.call-done), kind=kOutput, calls=%fused_computation.25 | convolution fusion | flops 8590458880 | bytes 26214400 | tf_op jit(solution)/shard_map/dot_general | solution.py:52
  291.2 0.3 copy.37
  291.5 0.0 slice-start
  291.5 2.5 fusion.10
  294.1 0.0 slice-done
  294.1 2.8 fusion.12
  296.9 0.5 fusion.65
  297.3 0.4 fusion.14
  297.7 0.8 fusion.8
  298.5 0.7 copy.25
  299.3 1.3 convert_element_type.134
  (18 shorter events, 0.2 us)
Async XLA Ops:
  6.5 2.8 copy-start.1
  6.5 46.3 %all-gather.12.cloned.1.call-start = ((), (), s32[]{:S(2)}) async-start(), calls=%async_computation.2 | async-start | bytes 2228224 | tf_op jit(solution)/shard_map/all_gather | solution.py:64
  7.3 130.9 %all-gather.8.cloned.1.call-start = ((), (), s32[]{:S(2)}) async-start(), calls=%async_computation | async-start | bytes 10485760 | tf_op jit(solution)/shard_map/all_gather | solution.py:49
  8.0 172.9 %all-gather.10.cloned.1.call-start = ((), (), s32[]{:S(2)}) async-start(), calls=%async_computation.1 | async-start | bytes 2228224 | tf_op jit(solution)/shard_map/all_gather | solution.py:59
  8.7 267.7 %all-gather.14.cloned.1.call-start = ((), (), s32[]{:S(2)}) async-start(), calls=%async_computation.3 | async-start | bytes 17825792 | tf_op jit(solution)/shard_map/all_gather | solution.py:54
  187.9 103.3 %copy-start = (f32[4,1,128,128]{3,2,0,1:T(8,128)}, f32[4,1,128,128]{3,2,0,1:T(8,128)S(1)}, u32[]{:S(2)}) copy-start(f32[4,1,128,128]{3,2,0,1:T(8,128)S(1)} %fusion.47) | copy-start | bytes 786436
  291.5 2.5 slice-start
Sparse Core Ops, SparseCore 0:
  9.2 43.6 all-gather.11
  54.6 83.4 all-gather.7
  139.9 40.9 all-gather.9
  182.6 93.7 all-gather.13
where the time goes:
time: 307 us
  waiting for transfers between devices  238 us (78%)
  matrix products  34.5 us (11%)
  blocking collectives  18.1 us (6%)
  between operations  13.3 us (4%)
    all_gather x1, waiting for transfers between devices, body(): features = lax.all_gather(hidden_in, 'head', axis=2, tiled=True)  85.3 us
    all_gather x1, waiting for transfers between devices, body(): lax.all_gather(w_query, 'dp', axis=0, tiled=True)  70 us
    all_gather x1, waiting for transfers between devices, body(): lax.all_gather(w_value, 'dp', axis=0, tiled=True)  43.4 us
    all_gather x1, waiting for transfers between devices, body(): lax.all_gather(w_key, 'dp', axis=0, tiled=True)  36.5 us
    all_gather x2, blocking collectives, entering(): lax.all_gather(part.astype(kind), axis)  18.1 us
    dot_general x1, matrix products, body(): jnp.dot(flattened, lax.all_gather(w_query, 'dp', axis=0, tiled=True), pre...  14.8 us
    dot_general x1, matrix products, body(): jnp.dot(flattened, lax.all_gather(w_key, 'dp', axis=0, tiled=True), prefe...  6.33 us
    dot_general x1, matrix products, body(): jnp.dot(flattened, lax.all_gather(w_value, 'dp', axis=0, tiled=True), pre...  6.3 us
  transfers between devices with their start and end apart: 4, of which 4 were waited for; matrix products, arithmetic and copies ran while one was open for 4% of the time, Pallas kernels for 0%

commit v1 on v0

--- a/solution.py
+++ b/solution.py
@@ -6,6 +6,33 @@
 
 HD = 128
 SEG = 128
+
+
+def detail_tasks(content, row_dim):
+    piece_out = list(content.shape[1:])
+    piece_out[row_dim] *= content.shape[0]
+    return jnp.moveaxis(content, 0, row_dim).reshape(piece_out)
+
+
+def register_rings(array_in, which_axis):
+    world = lax.axis_size(which_axis)
+    block_now = array_in[None]
+    for to_i in range(world.bit_length() - 1):
+        built = 1 << to_i
+        crops = []
+        for dd in range(world):
+            crops.append((dd, dd ^ built))
+        state_now = lax.ppermute(block_now, axis_name=which_axis, perm=crops)
+        item_now = jnp.stack([block_now, state_now])
+        q_next = lax.axis_index(which_axis)
+        newest = q_next >> to_i & 1
+        block_now = jnp.where(newest == 0, item_now, item_now[::-1]).reshape(-1, *array_in.shape)
+    return block_now
+
+
+def derive_tasks(local_x, z, which_dim):
+    fresh = register_rings(local_x, z)
+    return detail_tasks(fresh, which_dim)
 
 
 def entering(shard, axis, combine, identity):
@@ -60,9 +87,7 @@
         preferred_element_type=jnp.float32,
     )
     values_full = jnp.dot(
-        flattened,
-        lax.all_gather(w_value, "dp", axis=0, tiled=True),
-        preferred_element_type=jnp.float32,
+        flattened, derive_tasks(w_value, "dp", 0), preferred_element_type=jnp.float32
     )
     query = query_full.astype(jnp.bfloat16)
     keys = keys_full.astype(jnp.bfloat16)

time: 307 us -> 268 us (0.87)
  waiting for transfers between devices: 238 us -> 187 us
  starting transfers between devices: 0.12 us -> 10.3 us
    all_gather x1, waiting for transfers between devices: 85.3 us -> 0.02 us  [body(): features = lax.all_gather(hidden_in, 'head', axis=2, tiled=True)]
    ppermute x0 -> x4, waiting for transfers between devices: none -> 78.1 us  [register_rings(): state_now = lax.ppermute(block_now, axis_name=which_axis, perm=crops)]
    all_gather x1 -> x0, waiting for transfers between devices: 43.4 us -> none  [body(): lax.all_gather(w_value, 'dp', axis=0, tiled=True)]
    ppermute x0 -> x4, starting transfers between devices: none -> 10.2 us  [register_rings(): state_now = lax.ppermute(block_now, axis_name=which_axis, perm=crops)]
  transfers between devices with their start and end apart: 4 -> 7, of which waited for: 4 -> 6; matrix products, arithmetic and copies ran while one was open for 4% -> 6% of each run, Pallas kernels for 0% -> 0%
where the time goes in v1:
time: 268 us
  waiting for transfers between devices  187 us (70%)
  matrix products  34.4 us (13%)
  blocking collectives  18.1 us (7%)
  between operations  13.3 us (5%)
  starting transfers between devices  10.3 us (4%)
    ppermute x4, waiting for transfers between devices, register_rings(): state_now = lax.ppermute(block_now, axis_name=which_axis, perm=crops)  78.1 us
    all_gather x1, waiting for transfers between devices, body(): lax.all_gather(w_query, 'dp', axis=0, tiled=True)  70.1 us
    all_gather x1, waiting for transfers between devices, body(): lax.all_gather(w_key, 'dp', axis=0, tiled=True)  36.5 us
    all_gather x2, blocking collectives, entering(): lax.all_gather(part.astype(kind), axis)  18.1 us
    dot_general x1, matrix products, body(): jnp.dot(flattened, lax.all_gather(w_query, 'dp', axis=0, tiled=True), pre...  14.8 us
    ppermute x4, starting transfers between devices, register_rings(): state_now = lax.ppermute(block_now, axis_name=which_axis, perm=crops)  10.2 us
    dot_general x1, matrix products, body(): jnp.dot(flattened, lax.all_gather(w_key, 'dp', axis=0, tiled=True), prefe...  6.33 us
    dot_general x1, matrix products, body(): jnp.dot(flattened, derive_tasks(w_value, 'dp', 0), preferred_element_type...  6.28 us
  transfers between devices with their start and end apart: 7, of which 6 were waited for; matrix products, arithmetic and copies ran while one was open for 6% of the time, Pallas kernels for 0%

profile of v1, /device:TPU:1, one launch (start us, length us, event | category | flops | bytes accessed | tf_op | source)
XLA Modules:
  0.0 267.5 jit_solution(13899732575108269139)
XLA Ops:
  6.5 0.7 all-gather.7.cloned.1.call-update
  7.3 0.7 all-gather.9.cloned.1.call-update
  8.1 0.7 all-gather.11.cloned.1.call-update
  8.8 3.3 %collective-permute-start = (bf16[1,512,128]{2,1,0:T(8,128)(2,1)S(1)}, bf16[1,512,128]{2,1,0:T(8,128)(2,1)S(1)}, u32[]{:S(2)}, u32[]{:S(2)}) collective-permute-start(bf16[1,512,128]{2,1,0:T(8,128)(2,1)S(1)} %bitcast.143), channel_id=1, source_target_pairs={{0,16},{16,0},{32,48},{48,32},{64,80},{80,64},{96,112},{112,96},{1... | collective-permute-start | bytes 393224 | tf_op jit(solution)/shard_map/ppermute | solution.py:25
  12.0 1.0 collective-permute-done
  13.2 7.5 %collective-permute-done.1 = bf16[2,512,128]{2,1,0:T(8,128)(2,1)S(1)} collective-permute-done((bf16[2,512,128]{2,1,0:T(8,128)(2,1)S(1)}, bf16[2,512,128]{2,1,0:T(8,128)(2,1)S(1)}, u32[]{:S(2)}, u32[]{:S(2)}) %collective-permute-start.1) | collective-permute-done | bytes 262176 | tf_op jit(solution)/shard_map/ppermute | solution.py:25
  20.9 1.7 collective-permute-start.2
  22.6 24.2 %collective-permute-done.2 = bf16[4,512,128]{2,1,0:T(8,128)(2,1)S(1)} collective-permute-done((bf16[4,512,128]{2,1,0:T(8,128)(2,1)S(1)}, bf16[4,512,128]{2,1,0:T(8,128)(2,1)S(1)}, u32[]{:S(2)}, u32[]{:S(2)}) %collective-permute-start.2) | collective-permute-done | bytes 524320 | tf_op jit(solution)/shard_map/ppermute | solution.py:25
  46.9 0.2 reverse_select_fusion.1
  47.1 5.1 %collective-permute-start.3 = (bf16[8,512,128]{2,1,0:T(8,128)(2,1)S(1)}, bf16[8,512,128]{2,1,0:T(8,128)(2,1)S(1)}, u32[]{:S(2)}, u32[]{:S(2)}) collective-permute-start(bf16[8,512,128]{2,1,0:T(8,128)(2,1)S(1)} %bitcast.129), channel_id=1, source_target_pairs={{0,128},{16,144},{32,160},{48,176},{64,192},{80,208},{96,224},{112... | collective-permute-start | bytes 3145736 | tf_op jit(solution)/shard_map/ppermute | solution.py:25
  52.3 45.5 %collective-permute-done.3 = bf16[8,512,128]{2,1,0:T(8,128)(2,1)S(1)} collective-permute-done((bf16[8,512,128]{2,1,0:T(8,128)(2,1)S(1)}, bf16[8,512,128]{2,1,0:T(8,128)(2,1)S(1)}, u32[]{:S(2)}, u32[]{:S(2)}) %collective-permute-start.3) | collective-permute-done | bytes 1048608 | tf_op jit(solution)/shard_map/ppermute | solution.py:25
  97.7 0.2 pad_maximum_fusion
  97.9 0.5 reverse_select_fusion
  98.5 6.3 %fusion.24 = bf16[128,512]{1,0:T(8,128)(2,1)S(1)} fusion(bf16[8192,128]{1,0:T(8,128)(2,1)S(1)} %bitcast.125, bf16[1,512,8192]{2,1,0:T(8,128)(2,1)} %all-gather.7.cloned.1.call-done), kind=kOutput, calls=%fused_computation.30 | convolution fusion | flops 1073807360 | bytes 10616832 | tf_op jit(solution)/shard_map/dot_general | solution.py:89
  104.8 36.5 %all-gather.9.cloned.1.call-done = bf16[8192,128]{1,0:T(8,128)(2,1)} async-done(((bf16[512,128]{1,0:T(8,128)(2,1)}), bf16[8192,128]{1,0:T(8,128)(2,1)}) %all-gather.9.cloned.1.call-update) | async-done | bytes 2097168 | tf_op jit(solution)/shard_map/all_gather | solution.py:86
  141.3 6.3 %fusion.42 = (bf16[128]{0:T(256)(128)(2,1)S(1)}, bf16[512,128]{1,0:T(8,128)(2,1)S(1)}) fusion(bf16[8192,128]{1,0:T(8,128)(2,1)} %all-gather.9.cloned.1.call-done, bf16[1,512,8192]{2,1,0:T(8,128)(2,1)} %all-gather.7.cloned.1.call-done), kind=kOutput, calls=%fused_computation.55 | convolution fusion | flops 1074200448 | bytes 10617088 | tf_op jit(solution)/shard_map/dot_general | solution.py:84
  147.6 0.5 fusion.69
  148.1 0.2 fusion.47
  148.2 0.1 fusion.45
  148.4 7.6 %all-gather.2 = bf16[4,1,128]{2,1,0:T(2,128)(2,1)S(1)} all-gather(bf16[1,1,128]{2,1,0:T(2,128)(2,1)S(1)} %bitcast.149), channel_id=3, replica_groups=mesh['dp'=16,'ctx'=4,'head'=4] {'ctx'}, dimensions={0}, use_global_device_ids=true | all-gather | bytes 1280 | tf_op jit(solution)/shard_map/all_gather | solution.py:41
  156.1 10.5 %all-gather = bf16[512,128]{1,0:T(8,128)(2,1)S(1)} all-gather(bf16[128,128]{1,0:T(8,128)(2,1)S(1)} %get-tuple-element.154), channel_id=2, replica_groups=mesh['dp'=16,'ctx'=4,'head'=4] {'ctx'}, dimensions={0}, use_global_device_ids=true | all-gather | bytes 163840 | tf_op jit(solution)/shard_map/all_gather | solution.py:41
  166.6 0.2 while.16
  166.8 70.1 %all-gather.11.cloned.1.call-done = bf16[8192,1024]{1,0:T(8,128)(2,1)} async-done(((bf16[512,1024]{1,0:T(8,128)(2,1)}), bf16[8192,1024]{1,0:T(8,128)(2,1)}) %all-gather.11.cloned.1.call-update) | async-done | bytes 16777232 | tf_op jit(solution)/shard_map/all_gather | solution.py:81
  236.9 14.8 %fusion.18 = bf16[64,8,8,128]{3,1,2,0:T(8,128)(2,1)S(1)} fusion(bf16[8192,1024]{1,0:T(8,128)(2,1)} %all-gather.11.cloned.1.call-done, bf16[1,512,8192]{2,1,0:T(8,128)(2,1)} %all-gather.7.cloned.1.call-done), kind=kOutput, calls=%fused_computation.28 | convolution fusion | flops 8590458880 | bytes 26214400 | tf_op jit(solution)/shard_map/dot_general | solution.py:79
  251.7 0.3 copy.41
  252.0 2.5 fusion.10
  254.5 2.8 %fusion.12 = f32[4,128,128,8]{2,1,3,0:T(8,128)S(1)} fusion(bf16[4,128,8,128]{3,2,1,0:T(8,128)(2,1)S(1)} %bitcast.127, f32[3,1,128,128]{3,2,0,1:T(8,128)S(1)} %slice-done, f32[128,128]{1,0:T(8,128)S(1)} %bitcast.133), kind=kOutput, calls=%fused_computation.24 | convolution fusion | flops 807993344 | bytes 3407872 | tf_op jit(solution)/shard_map/nqkgd,nkde->nqkge/dot_general | solution.py:124
  257.3 0.5 fusion.70
  257.7 0.4 fusion.14
  258.1 0.8 fusion.8
  259.0 0.7 copy.28
  259.7 1.3 convert_element_type.138
  (34 shorter events, 0.8 us)
Async XLA Ops:
  6.5 2.2 copy-start.1
  6.5 92.0 %all-gather.7.cloned.1.call-start = ((), (), s32[]{:S(2)}) async-start(), calls=%async_computation | async-start | bytes 10485760 | tf_op jit(solution)/shard_map/all_gather | solution.py:76
  7.3 134.0 %all-gather.9.cloned.1.call-start = ((), (), s32[]{:S(2)}) async-start(), calls=%async_computation.1 | async-start | bytes 2228224 | tf_op jit(solution)/shard_map/all_gather | solution.py:86
  8.0 228.9 %all-gather.11.cloned.1.call-start = ((), (), s32[]{:S(2)}) async-start(), calls=%async_computation.2 | async-start | bytes 17825792 | tf_op jit(solution)/shard_map/all_gather | solution.py:81
  8.8 4.3 %collective-permute-start = (bf16[1,512,128]{2,1,0:T(8,128)(2,1)S(1)}, bf16[1,512,128]{2,1,0:T(8,128)(2,1)S(1)}, u32[]{:S(2)}, u32[]{:S(2)}) collective-permute-start(bf16[1,512,128]{2,1,0:T(8,128)(2,1)S(1)} %bitcast.143), channel_id=1, source_target_pairs={{0,16},{16,0},{32,48},{48,32},{64,80},{80,64},{96,112},{112,96},{1... | collective-permute-start | bytes 393224 | tf_op jit(solution)/shard_map/ppermute | solution.py:25
  13.1 7.6 %collective-permute-start.1 = (bf16[2,512,128]{2,1,0:T(8,128)(2,1)S(1)}, bf16[2,512,128]{2,1,0:T(8,128)(2,1)S(1)}, u32[]{:S(2)}, u32[]{:S(2)}) collective-permute-start(bf16[2,512,128]{2,1,0:T(8,128)(2,1)S(1)} %get-tuple-element.153), channel_id=1, source_target_pairs={{0,32},{16,48},{32,0},{48,16},{64,96},{80,112},{96,64},{112,80},{1... | collective-permute-start | bytes 786440 | tf_op jit(solution)/shard_map/ppermute | solution.py:25
  20.9 25.9 %collective-permute-start.2 = (bf16[4,512,128]{2,1,0:T(8,128)(2,1)S(1)}, bf16[4,512,128]{2,1,0:T(8,128)(2,1)S(1)}, u32[]{:S(2)}, u32[]{:S(2)}) collective-permute-start(bf16[4,512,128]{2,1,0:T(8,128)(2,1)S(1)} %bitcast.131), channel_id=1, source_target_pairs={{0,64},{16,80},{32,96},{48,112},{64,0},{80,16},{96,32},{112,48},{1... | collective-permute-start | bytes 1572872 | tf_op jit(solution)/shard_map/ppermute | solution.py:25
  46.8 5.5 %copy-start.2 = (f32[8]{0:T(128)S(1)}, f32[8]{0:T(128)}, u32[]{:S(2)}) copy-start(f32[8]{0:T(128)} %param.11) | copy-start | bytes 100
  47.1 50.6 %collective-permute-start.3 = (bf16[8,512,128]{2,1,0:T(8,128)(2,1)S(1)}, bf16[8,512,128]{2,1,0:T(8,128)(2,1)S(1)}, u32[]{:S(2)}, u32[]{:S(2)}) collective-permute-start(bf16[8,512,128]{2,1,0:T(8,128)(2,1)S(1)} %bitcast.129), channel_id=1, source_target_pairs={{0,128},{16,144},{32,160},{48,176},{64,192},{80,208},{96,224},{112... | collective-permute-start | bytes 3145736 | tf_op jit(solution)/shard_map/ppermute | solution.py:25
  148.2 103.4 %copy-start = (f32[4,1,128,128]{3,2,0,1:T(8,128)}, f32[4,1,128,128]{3,2,0,1:T(8,128)S(1)}, u32[]{:S(2)}) copy-start(f32[4,1,128,128]{3,2,0,1:T(8,128)S(1)} %fusion.47) | copy-start | bytes 786436
  251.9 2.5 slice-start
Sparse Core Ops, SparseCore 0:
  9.1 89.2 all-gather.6
  100.3 40.9 all-gather.8
  143.1 93.7 all-gather.10
